TPU v7x, 32 devices: a whole 2x2x4 slice. The times are simulated.
32 devices in a mesh: gx: 8 (over z, core), gy: 4 (over y, x).
Axes of the slice: x: 2, y: 2, z: 4, core: 2. Of those that a mesh axis runs over, the one named last changes fastest.
Arguments:
- blocks: bfloat16 [8, 4, 3, 320, 2240], P('gx', 'gy'), may hold values from -1 to 2
- right_side: bfloat16 [8, 4, 3, 320, 128], P('gx', 'gy'), may hold values from -6 to 6
- departure: int32 [8, 4, 2], P('gx', 'gy'), may hold values from -1 to 2, as said below
- arrival: int32 [8, 4, 2], P('gx', 'gy'), may hold values from 0 to 4, as said below
- neighbors: int32 [8, 4, 2, 6], P('gx', 'gy'), may hold values from 0 to 5, as said below
- orientation: int32 [8, 4, 2, 6], P('gx', 'gy'), may hold values from 0 to 3
Outputs:
- smoothed: float32 [8, 4, 2, 320, 128], P('gx', 'gy')
Inputs may be any that keep to these rules, and one draw needn't show every extreme that they name: Position (l, c) holds its rows in some of its 3 slots; its live slots are exactly those named in its departure or arrival entries, each once. At most one of the two entries is a slot; the device with c = 0 never sends lower, the one with c = 3 never upper. Every position holds 1 to 3 rows before and exactly 2 after; in every layer some position holds 3. `arrival`: values below 3 name a local slot, kept in rising order; 3 is the row that the lower gy neighbour sends upward, 4 the one the upper neighbour sends downward, consistent with departure. `neighbors`: face 0 names 0 or 1, face 1 names 4 or 5; no entry of row q names 2 + q.
All inputs are finite; a program needn't handle non-finite values.
Results may differ from a plain program's by a relative error of at most 0.0035.
Values may be sent and summed in bfloat16 or wider, within the bound.
A program may use at most 64 MiB of HBM per device.

v0:
```python
import jax
import jax.numpy as jnp
from jax import lax
from jax.sharding import PartitionSpec as P

NODES = 4
ITERS = 4


RELAXATION = 0.7


def with_halo(block, sides, width):
    for axis, dim in sides:
        count = lax.axis_size(axis)
        forward = [(i, i + 1) for i in range(count - 1)]
        backward = [(target, source) for source, target in forward]
        low = lax.ppermute(
            lax.slice_in_dim(block, block.shape[dim] - width, None, axis=dim), axis, forward
        )
        high = lax.ppermute(lax.slice_in_dim(block, 0, width, axis=dim), axis, backward)
        block = jnp.concatenate([low, block, high], axis=dim)
    return block


def from_behind(value, axis, steps):
    count = lax.axis_size(axis)
    leading, last = (max(0, -steps), min(count, count - steps))
    return lax.ppermute(value, axis, [(source, source + steps) for source in range(leading, last)])


def turned_faces(faces, face_codes):
    row_count, face_count, dof_width, rhs_width = faces.shape
    nodal = faces.reshape(
        row_count, face_count, dof_width // NODES**3, NODES, NODES, NODES, rhs_width
    )
    result = nodal
    for quarter in range(1, 4):
        result = jnp.where(
            (face_codes == quarter)[:, :, None, None, None, None, None],
            jnp.rot90(nodal, quarter, axes=(3, 4)),
            result,
        )
    return result.reshape(row_count, face_count, dof_width, rhs_width)


def coupled(row_blocks, window, face_links, face_codes, own_rows):
    faces = turned_faces(jnp.take(window, face_links, axis=0), face_codes)
    stacked = jnp.concatenate([own_rows[:, None], faces], axis=1)
    stacked = stacked.reshape(stacked.shape[0], -1, stacked.shape[-1])
    return jnp.einsum("nde,ner->ndr", row_blocks, stacked, preferred_element_type=jnp.float32)


def layer_window(rounded):
    lifted = with_halo(rounded[None], (("gx", 0),), 1)
    return lifted.reshape(-1, rounded.shape[1], rounded.shape[2])


def shards(blocks, right_side, departure, arrival, neighbors, orientation):
    local_blocks = blocks[0, 0]
    local_rhs = right_side[0, 0]
    leaving_slots = departure[0, 0]
    sources = arrival[0, 0]
    face_links = neighbors[0, 0]
    face_codes = orientation[0, 0]
    lower_slot = jnp.maximum(leaving_slots[0], 0)
    upper_slot = jnp.maximum(leaving_slots[1], 0)
    from_upper = from_behind((local_blocks[lower_slot], local_rhs[lower_slot]), "gy", -1)
    from_lower = from_behind((local_blocks[upper_slot], local_rhs[upper_slot]), "gy", 1)
    block_pool = jnp.concatenate([local_blocks, from_lower[0][None], from_upper[0][None]], axis=0)
    rhs_pool = jnp.concatenate([local_rhs, from_lower[1][None], from_upper[1][None]], axis=0)
    kept_blocks = jnp.take(block_pool, sources, axis=0)
    kept_rhs = jnp.take(rhs_pool, sources, axis=0).astype(jnp.float32)
    current = RELAXATION * kept_rhs
    for sweep_index in range(ITERS):
        rounded = current.astype(jnp.bfloat16)
        window = layer_window(rounded)
        applied = coupled(kept_blocks, window, face_links, face_codes, rounded)
        current = current + RELAXATION * (kept_rhs - applied)
    return current[None, None]


def solution(mesh):
    in_specs = (
        P("gx", "gy", None, None, None),
        P("gx", "gy", None, None, None),
        P("gx", "gy", None),
        P("gx", "gy", None),
        P("gx", "gy", None, None),
        P("gx", "gy", None, None),
    )
    out_specs = P("gx", "gy", None, None, None)
    return jax.shard_map(shards, mesh=mesh, in_specs=in_specs, out_specs=out_specs, check_vma=False)
```

profile of v0, /device:TPU:11, one launch (start us, length us, event | category | flops | bytes accessed | tf_op | source)
XLA Modules:
  0.0 132.8 jit_solution(3957047420490651517)
XLA Ops:
  0.0 1.3 fusion.19
  2.5 1.0 dynamic-slice_bitcast_fusion.3
  3.5 3.1 %collective-permute-start = (bf16[320,128]{1,0:T(8,128)(2,1)S(1)}, bf16[320,128]{1,0:T(8,128)(2,1)S(1)}, u32[]{:S(2)}, u32[]{:S(2)}) collective-permute-start(bf16[320,128]{1,0:T(8,128)(2,1)S(1)} %get-tuple-element.22), channel_id=1, source_target_pairs={{0,1},{1,2},{2,3},{4,5},{5,6},{6,7},{8,9},{9,10},{10,11},{12,13},{... | collective-permute-start | bytes 245768 | tf_op jit(solution)/shard_map/ppermute | solution.py:29
  6.7 2.3 %collective-permute-start.1 = (bf16[320,128]{1,0:T(8,128)(2,1)S(1)}, bf16[320,128]{1,0:T(8,128)(2,1)S(1)}, u32[]{:S(2)}, u32[]{:S(2)}) collective-permute-start(bf16[320,128]{1,0:T(8,128)(2,1)S(1)} %get-tuple-element.23), channel_id=1, source_target_pairs={{1,0},{2,1},{3,2},{5,4},{6,5},{7,6},{9,8},{10,9},{11,10},{13,12},{... | collective-permute-start | bytes 245768 | tf_op jit(solution)/shard_map/ppermute | solution.py:29
  9.0 3.7 %dynamic-slice_bitcast_fusion.1 = (bf16[320,2240]{1,0:T(8,128)(2,1)}, bf16[320,2240]{1,0:T(8,128)(2,1)}) fusion(bf16[1,1,3,320,2240]{4,3,2,1,0:T(8,128)(2,1)} %param.8, s32[]{:T(128)} %bitcast.2, s32[]{:T(128)} %bitcast.5), kind=kLoop, calls=%fused_computation.9 | loop fusion | bytes 5734408 | tf_op jit(solution)/shard_map/squeeze | solution.py:69
  12.7 4.0 %collective-permute-start.2 = (bf16[320,2240]{1,0:T(8,128)(2,1)}, bf16[320,2240]{1,0:T(8,128)(2,1)S(1)}, u32[]{:S(2)}, u32[]{:S(2)}) collective-permute-start(bf16[320,2240]{1,0:T(8,128)(2,1)} %get-tuple-element.6), channel_id=1, source_target_pairs={{0,1},{1,2},{2,3},{4,5},{5,6},{6,7},{8,9},{9,10},{10,11},{12,13},{... | collective-permute-start | bytes 4300808 | tf_op jit(solution)/shard_map/ppermute | solution.py:29
  16.7 1.9 %collective-permute-start.3 = (bf16[320,2240]{1,0:T(8,128)(2,1)}, bf16[320,2240]{1,0:T(8,128)(2,1)}, u32[]{:S(2)}, u32[]{:S(2)}) collective-permute-start(bf16[320,2240]{1,0:T(8,128)(2,1)} %get-tuple-element.7), channel_id=1, source_target_pairs={{1,0},{2,1},{3,2},{5,4},{6,5},{7,6},{9,8},{10,9},{11,10},{13,12},{... | collective-permute-start | bytes 4300808 | tf_op jit(solution)/shard_map/ppermute | solution.py:29
  18.9 0.6 gather_fusion
  19.6 3.3 %collective-permute-start.5 = (bf16[1,2,320,128]{3,2,1,0:T(8,128)(2,1)S(1)}, bf16[1,2,320,128]{3,2,1,0:T(8,128)(2,1)S(1)}, u32[]{:S(2)}, u32[]{:S(2)}) collective-permute-start(bf16[1,2,320,128]{3,2,1,0:T(8,128)(2,1)S(1)} %multiply_convert_fusion), channel_id=1, source_target_pairs={{4,0},{8,4},{12,8},{16,12},{20,16},{24,20},{28,24},{5,1},{9,5},{13... | collective-permute-start | bytes 491528 | tf_op jit(solution)/shard_map/ppermute | solution.py:21
  22.9 3.2 %collective-permute-start.4 = (bf16[1,2,320,128]{3,2,1,0:T(8,128)(2,1)S(1)}, bf16[1,2,320,128]{3,2,1,0:T(8,128)(2,1)S(1)}, u32[]{:S(2)}, u32[]{:S(2)}) collective-permute-start(bf16[1,2,320,128]{3,2,1,0:T(8,128)(2,1)S(1)} %multiply_convert_fusion), channel_id=1, source_target_pairs={{0,4},{4,8},{8,12},{12,16},{16,20},{20,24},{24,28},{1,5},{5,9},{9,... | collective-permute-start | bytes 491528 | tf_op jit(solution)/shard_map/ppermute | solution.py:18
  26.2 1.2 collective-permute-done.5
  27.5 0.9 collective-permute-done.4
  28.4 0.7 gather_fusion.2
  29.3 0.4 copy.58
  29.8 1.4 %fusion.16 = bf16[2,6,5,4,4,4,128]{6,5,4,3,2,1,0:T(4,128)(2,1)S(1)} fusion(bf16[2,6,5,4,4,4,128]{6,5,4,3,2,1,0:T(4,128)(2,1)S(1)} %bitcast.129, bf16[2,6,5,4,4,4,128]{6,5,3,4,2,1,0:T(4,128)(2,1)S(1)} %copy.58, bf16[2,6,5,4,4,4,128]{6,5,4,3,2,1,0:T(4,128)(2,1)S(1)} %bitcast.130, pred[2,6]{1,0:T(4,128)(4,1)S(1)} %get-tuple-element.25, ...), kind=kLoop, calls=%fused_computation.38 | loop fusion | flops 1474560 | bytes 3932196 | tf_op jit(solution)/shard_map/jit(_where)/select_n | solution.py:39
  31.2 1.1 pad_maximum_fusion.1
  32.3 15.2 %collective-permute-done.2 = bf16[320,2240]{1,0:T(8,128)(2,1)S(1)} collective-permute-done((bf16[320,2240]{1,0:T(8,128)(2,1)}, bf16[320,2240]{1,0:T(8,128)(2,1)S(1)}, u32[]{:S(2)}, u32[]{:S(2)}) %collective-permute-start.2) | collective-permute-done | bytes 1433632 | tf_op jit(solution)/shard_map/ppermute | solution.py:29
  47.5 32.6 %collective-permute-done.3 = bf16[320,2240]{1,0:T(8,128)(2,1)} collective-permute-done((bf16[320,2240]{1,0:T(8,128)(2,1)}, bf16[320,2240]{1,0:T(8,128)(2,1)}, u32[]{:S(2)}, u32[]{:S(2)}) %collective-permute-start.3) | collective-permute-done | bytes 1433632 | tf_op jit(solution)/shard_map/ppermute | solution.py:29
  80.0 5.0 %pad_maximum_fusion = bf16[5,320,2240]{2,1,0:T(8,128)(2,1)} fusion(bf16[1,320,2240]{2,1,0:T(8,128)(2,1)} %bitcast.14, bf16[1,320,2240]{2,1,0:T(8,128)(2,1)S(1)} %bitcast.149, bf16[3,320,2240]{2,1,0:T(8,128)(2,1)S(1)} %bitcast.124), kind=kLoop, calls=%fused_computation.6 | loop fusion | flops 7168000 | bytes 14336000 | tf_op jit(solution)/shard_map/concatenate | solution.py:70
  85.0 3.8 %gather_fusion.1 = bf16[2,320,2240]{2,1,0:T(8,128)(2,1)S(1)} fusion(bf16[5,320,2240]{2,1,0:T(8,128)(2,1)} %pad_maximum_fusion, s32[1024]{0:T(1024)S(1)} %pad_clamp_fusion.1), kind=kCustom, calls=%fused_computation.5 | custom fusion | bytes 5734408 | tf_op jit(solution)/shard_map/jit(_take)/gather | solution.py:72
  88.9 3.1 %fusion.1 = f32[2,320,128]{2,1,0:T(8,128)S(1)} fusion(bf16[2,2240,128]{2,1,0:T(8,128)(2,1)} %bitcast.150, bf16[2,320,128]{2,1,0:T(8,128)(2,1)S(1)} %gather_fusion, pred[2]{0:T(512)(128)(4,1)S(1)} %compare_and_fusion.1, bf16[2,320,2240]{2,1,0:T(8,128)(2,1)S(1)} %gather_fusion.1), kind=kOutput, calls=%fused_computation.15 | convolution fusion | flops 368844800 | bytes 4505602 | tf_op jit(solution)/shard_map/nde,ner->ndr/dot_general | solution.py:51
  92.0 4.0 %collective-permute-start.7 = (bf16[1,2,320,128]{3,2,1,0:T(8,128)(2,1)S(1)}, bf16[1,2,320,128]{3,2,1,0:T(8,128)(2,1)S(1)}, u32[]{:S(2)}, u32[]{:S(2)}) collective-permute-start(bf16[1,2,320,128]{3,2,1,0:T(8,128)(2,1)S(1)} %get-tuple-element.21), channel_id=1, source_target_pairs={{4,0},{8,4},{12,8},{16,12},{20,16},{24,20},{28,24},{5,1},{9,5},{13... | collective-permute-start | bytes 491528 | tf_op jit(solution)/shard_map/ppermute | solution.py:21
  96.1 3.1 %collective-permute-start.6 = (bf16[1,2,320,128]{3,2,1,0:T(8,128)(2,1)S(1)}, bf16[1,2,320,128]{3,2,1,0:T(8,128)(2,1)S(1)}, u32[]{:S(2)}, u32[]{:S(2)}) collective-permute-start(bf16[1,2,320,128]{3,2,1,0:T(8,128)(2,1)S(1)} %get-tuple-element.21), channel_id=1, source_target_pairs={{0,4},{4,8},{8,12},{12,16},{16,20},{20,24},{24,28},{1,5},{5,9},{9,... | collective-permute-start | bytes 491528 | tf_op jit(solution)/shard_map/ppermute | solution.py:18
  99.2 1.1 collective-permute-done.7
  100.2 1.2 collective-permute-done.6
  101.5 0.7 gather_fusion.3
  102.4 0.4 copy.57
  102.8 1.4 %fusion.14 = bf16[2,6,5,4,4,4,128]{6,5,4,3,2,1,0:T(4,128)(2,1)S(1)} fusion(bf16[2,6,5,4,4,4,128]{6,5,4,3,2,1,0:T(4,128)(2,1)S(1)} %bitcast.132, bf16[2,6,5,4,4,4,128]{6,5,3,4,2,1,0:T(4,128)(2,1)S(1)} %copy.57, bf16[2,6,5,4,4,4,128]{6,5,4,3,2,1,0:T(4,128)(2,1)S(1)} %bitcast.135, pred[2,6]{1,0:T(4,128)(4,1)S(1)} %get-tuple-element.25, ...), kind=kLoop, calls=%fused_computation.35 | loop fusion | flops 1474560 | bytes 3932196 | tf_op jit(solution)/shard_map/jit(_where)/select_n | solution.py:39
  104.7 0.7 copy-done.6
  105.3 1.0 fusion.3
  106.4 3.2 %collective-permute-start.9 = (bf16[1,2,320,128]{3,2,1,0:T(8,128)(2,1)S(1)}, bf16[1,2,320,128]{3,2,1,0:T(8,128)(2,1)S(1)}, u32[]{:S(2)}, u32[]{:S(2)}) collective-permute-start(bf16[1,2,320,128]{3,2,1,0:T(8,128)(2,1)S(1)} %get-tuple-element.19), channel_id=1, source_target_pairs={{4,0},{8,4},{12,8},{16,12},{20,16},{24,20},{28,24},{5,1},{9,5},{13... | collective-permute-start | bytes 491528 | tf_op jit(solution)/shard_map/ppermute | solution.py:21
  109.6 3.1 %collective-permute-start.8 = (bf16[1,2,320,128]{3,2,1,0:T(8,128)(2,1)S(1)}, bf16[1,2,320,128]{3,2,1,0:T(8,128)(2,1)S(1)}, u32[]{:S(2)}, u32[]{:S(2)}) collective-permute-start(bf16[1,2,320,128]{3,2,1,0:T(8,128)(2,1)S(1)} %get-tuple-element.19), channel_id=1, source_target_pairs={{0,4},{4,8},{8,12},{12,16},{16,20},{20,24},{24,28},{1,5},{5,9},{9,... | collective-permute-start | bytes 491528 | tf_op jit(solution)/shard_map/ppermute | solution.py:18
  112.7 1.1 collective-permute-done.9
  113.8 1.2 collective-permute-done.8
  115.0 0.7 gather_fusion.4
  115.9 0.4 copy.56
  116.4 1.4 %fusion.12 = bf16[2,6,5,4,4,4,128]{6,5,4,3,2,1,0:T(4,128)(2,1)S(1)} fusion(bf16[2,6,5,4,4,4,128]{6,5,4,3,2,1,0:T(4,128)(2,1)S(1)} %bitcast.134, bf16[2,6,5,4,4,4,128]{6,5,3,4,2,1,0:T(4,128)(2,1)S(1)} %copy.56, bf16[2,6,5,4,4,4,128]{6,5,4,3,2,1,0:T(4,128)(2,1)S(1)} %bitcast.136, pred[2,6]{1,0:T(4,128)(4,1)S(1)} %get-tuple-element.25, ...), kind=kLoop, calls=%fused_computation.32 | loop fusion | flops 1474560 | bytes 3932196 | tf_op jit(solution)/shard_map/jit(_where)/select_n | solution.py:39
  117.9 0.3 copy-done.2
  118.2 1.0 fusion.5
  119.2 3.2 %collective-permute-start.11 = (bf16[1,2,320,128]{3,2,1,0:T(8,128)(2,1)S(1)}, bf16[1,2,320,128]{3,2,1,0:T(8,128)(2,1)S(1)}, u32[]{:S(2)}, u32[]{:S(2)}) collective-permute-start(bf16[1,2,320,128]{3,2,1,0:T(8,128)(2,1)S(1)} %get-tuple-element.17), channel_id=1, source_target_pairs={{4,0},{8,4},{12,8},{16,12},{20,16},{24,20},{28,24},{5,1},{9,5},{13... | collective-permute-start | bytes 491528 | tf_op jit(solution)/shard_map/ppermute | solution.py:21
  122.4 3.3 %collective-permute-start.10 = (bf16[1,2,320,128]{3,2,1,0:T(8,128)(2,1)S(1)}, bf16[1,2,320,128]{3,2,1,0:T(8,128)(2,1)S(1)}, u32[]{:S(2)}, u32[]{:S(2)}) collective-permute-start(bf16[1,2,320,128]{3,2,1,0:T(8,128)(2,1)S(1)} %get-tuple-element.17), channel_id=1, source_target_pairs={{0,4},{4,8},{8,12},{12,16},{16,20},{20,24},{24,28},{1,5},{5,9},{9,... | collective-permute-start | bytes 491528 | tf_op jit(solution)/shard_map/ppermute | solution.py:18
  125.7 0.9 collective-permute-done.11
  126.6 1.2 collective-permute-done.10
  127.9 0.7 gather_fusion.5
  128.8 0.4 copy.55
  129.2 1.4 %fusion.10 = bf16[2,6,5,4,4,4,128]{6,5,4,3,2,1,0:T(4,128)(2,1)S(1)} fusion(bf16[2,6,5,4,4,4,128]{6,5,4,3,2,1,0:T(4,128)(2,1)S(1)} %bitcast.126, bf16[2,6,5,4,4,4,128]{6,5,3,4,2,1,0:T(4,128)(2,1)S(1)} %copy.55, bf16[2,6,5,4,4,4,128]{6,5,4,3,2,1,0:T(4,128)(2,1)S(1)} %bitcast.127, pred[2,6]{1,0:T(4,128)(4,1)S(1)} %get-tuple-element.25, ...), kind=kLoop, calls=%fused_computation.29 | loop fusion | flops 1474560 | bytes 3932196 | tf_op jit(solution)/shard_map/jit(_where)/select_n | solution.py:39
  130.7 0.3 copy-done.3
  131.0 1.7 %fusion.8 = f32[1,1,2,320,128]{4,3,2,1,0:T(8,128)} fusion(f32[2,320,128]{2,1,0:T(8,128)S(1)} %fusion.5, bf16[2,2240,128]{2,1,0:T(8,128)(2,1)S(1)} %bitcast.151, bf16[2,320,128]{2,1,0:T(8,128)(2,1)S(1)} %gather_fusion, pred[2]{0:T(512)(128)(4,1)S(1)} %compare_and_fusion.1, bf16[2,320,2240]{2,1,0:T(8,128)(2,1)S(1)} %copy-done.3), kind=kOutput, calls=%fused_computation.22 | convolution fusion | flops 368844800 | bytes 4833282 | tf_op jit(solution)/shard_map/nde,ner->ndr/dot_general | solution.py:51
  (49 shorter events, 2.0 us)
Async XLA Ops:
  3.5 15.3 %collective-permute-start = (bf16[320,128]{1,0:T(8,128)(2,1)S(1)}, bf16[320,128]{1,0:T(8,128)(2,1)S(1)}, u32[]{:S(2)}, u32[]{:S(2)}) collective-permute-start(bf16[320,128]{1,0:T(8,128)(2,1)S(1)} %get-tuple-element.22), channel_id=1, source_target_pairs={{0,1},{1,2},{2,3},{4,5},{5,6},{6,7},{8,9},{9,10},{10,11},{12,13},{... | collective-permute-start | bytes 245768 | tf_op jit(solution)/shard_map/ppermute | solution.py:29
  6.6 12.0 %copy-start.9 = (s32[1,1,2]{2,1,0:T(1,128)S(1)}, s32[1,1,2]{2,1,0:T(1,128)}, u32[]{:S(2)}) copy-start(s32[1,1,2]{2,1,0:T(1,128)} %param.11) | copy-start | bytes 28
  6.7 12.0 %copy-start.7 = (s32[1,1,2,6]{3,2,1,0:T(2,128)S(1)}, s32[1,1,2,6]{3,2,1,0:T(2,128)}, u32[]{:S(2)}) copy-start(s32[1,1,2,6]{3,2,1,0:T(2,128)} %param.12) | copy-start | bytes 148
  6.7 12.1 %copy-start.8 = (s32[1,1,2,6]{3,2,1,0:T(2,128)S(1)}, s32[1,1,2,6]{3,2,1,0:T(2,128)}, u32[]{:S(2)}) copy-start(s32[1,1,2,6]{3,2,1,0:T(2,128)} %param.13) | copy-start | bytes 148
  6.7 12.1 %copy-start.4 = (bf16[1,1,3,320,128]{4,3,2,1,0:T(8,128)(2,1)S(1)}, bf16[1,1,3,320,128]{4,3,2,1,0:T(8,128)(2,1)}, u32[]{:S(2)}) copy-start(bf16[1,1,3,320,128]{4,3,2,1,0:T(8,128)(2,1)} %param.9) | copy-start | bytes 737284
  6.7 12.1 %collective-permute-start.1 = (bf16[320,128]{1,0:T(8,128)(2,1)S(1)}, bf16[320,128]{1,0:T(8,128)(2,1)S(1)}, u32[]{:S(2)}, u32[]{:S(2)}) collective-permute-start(bf16[320,128]{1,0:T(8,128)(2,1)S(1)} %get-tuple-element.23), channel_id=1, source_target_pairs={{1,0},{2,1},{3,2},{5,4},{6,5},{7,6},{9,8},{10,9},{11,10},{13,12},{... | collective-permute-start | bytes 245768 | tf_op jit(solution)/shard_map/ppermute | solution.py:29
  12.7 34.8 %collective-permute-start.2 = (bf16[320,2240]{1,0:T(8,128)(2,1)}, bf16[320,2240]{1,0:T(8,128)(2,1)S(1)}, u32[]{:S(2)}, u32[]{:S(2)}) collective-permute-start(bf16[320,2240]{1,0:T(8,128)(2,1)} %get-tuple-element.6), channel_id=1, source_target_pairs={{0,1},{1,2},{2,3},{4,5},{5,6},{6,7},{8,9},{9,10},{10,11},{12,13},{... | collective-permute-start | bytes 4300808 | tf_op jit(solution)/shard_map/ppermute | solution.py:29
  16.7 63.3 %collective-permute-start.3 = (bf16[320,2240]{1,0:T(8,128)(2,1)}, bf16[320,2240]{1,0:T(8,128)(2,1)}, u32[]{:S(2)}, u32[]{:S(2)}) collective-permute-start(bf16[320,2240]{1,0:T(8,128)(2,1)} %get-tuple-element.7), channel_id=1, source_target_pairs={{1,0},{2,1},{3,2},{5,4},{6,5},{7,6},{9,8},{10,9},{11,10},{13,12},{... | collective-permute-start | bytes 4300808 | tf_op jit(solution)/shard_map/ppermute | solution.py:29
  19.6 7.9 %collective-permute-start.5 = (bf16[1,2,320,128]{3,2,1,0:T(8,128)(2,1)S(1)}, bf16[1,2,320,128]{3,2,1,0:T(8,128)(2,1)S(1)}, u32[]{:S(2)}, u32[]{:S(2)}) collective-permute-start(bf16[1,2,320,128]{3,2,1,0:T(8,128)(2,1)S(1)} %multiply_convert_fusion), channel_id=1, source_target_pairs={{4,0},{8,4},{12,8},{16,12},{20,16},{24,20},{28,24},{5,1},{9,5},{13... | collective-permute-start | bytes 491528 | tf_op jit(solution)/shard_map/ppermute | solution.py:21
  22.9 5.4 %collective-permute-start.4 = (bf16[1,2,320,128]{3,2,1,0:T(8,128)(2,1)S(1)}, bf16[1,2,320,128]{3,2,1,0:T(8,128)(2,1)S(1)}, u32[]{:S(2)}, u32[]{:S(2)}) collective-permute-start(bf16[1,2,320,128]{3,2,1,0:T(8,128)(2,1)S(1)} %multiply_convert_fusion), channel_id=1, source_target_pairs={{0,4},{4,8},{8,12},{12,16},{16,20},{20,24},{24,28},{1,5},{5,9},{9,... | collective-permute-start | bytes 491528 | tf_op jit(solution)/shard_map/ppermute | solution.py:18
  28.4 51.7 %slice-start = ((s8[4423680]{0:T(1024)(128)(4,1)}), s8[229376]{0:T(1024)(128)(4,1)S(1)}, s32[]{:S(2)}) async-start(s8[4423680]{0:T(1024)(128)(4,1)} %bitcast.122), calls=%async_computation | async-start | bytes 458752
  29.3 50.7 %slice-start.1 = ((s8[4423680]{0:T(1024)(128)(4,1)}), s8[4194304]{0:T(1024)(128)(4,1)S(1)}, s32[]{:S(2)}) async-start(s8[4423680]{0:T(1024)(128)(4,1)} %bitcast.122), calls=%async_computation.1 | async-start | bytes 8388608
  88.9 3.1 %copy-start = (bf16[2,320,2240]{2,1,0:T(8,128)(2,1)}, bf16[2,320,2240]{2,1,0:T(8,128)(2,1)S(1)}, u32[]{:S(2)}) copy-start(bf16[2,320,2240]{2,1,0:T(8,128)(2,1)S(1)} %gather_fusion.1) | copy-start | bytes 8601604
  92.0 9.5 %copy-start.5 = (f32[2,320,128]{2,1,0:T(8,128)}, f32[2,320,128]{2,1,0:T(8,128)S(1)}, u32[]{:S(2)}) copy-start(f32[2,320,128]{2,1,0:T(8,128)S(1)} %fusion.1) | copy-start | bytes 983044
  92.0 8.2 %collective-permute-start.7 = (bf16[1,2,320,128]{3,2,1,0:T(8,128)(2,1)S(1)}, bf16[1,2,320,128]{3,2,1,0:T(8,128)(2,1)S(1)}, u32[]{:S(2)}, u32[]{:S(2)}) collective-permute-start(bf16[1,2,320,128]{3,2,1,0:T(8,128)(2,1)S(1)} %get-tuple-element.21), channel_id=1, source_target_pairs={{4,0},{8,4},{12,8},{16,12},{20,16},{24,20},{28,24},{5,1},{9,5},{13... | collective-permute-start | bytes 491528 | tf_op jit(solution)/shard_map/ppermute | solution.py:21
  96.1 5.4 %collective-permute-start.6 = (bf16[1,2,320,128]{3,2,1,0:T(8,128)(2,1)S(1)}, bf16[1,2,320,128]{3,2,1,0:T(8,128)(2,1)S(1)}, u32[]{:S(2)}, u32[]{:S(2)}) collective-permute-start(bf16[1,2,320,128]{3,2,1,0:T(8,128)(2,1)S(1)} %get-tuple-element.21), channel_id=1, source_target_pairs={{0,4},{4,8},{8,12},{12,16},{16,20},{20,24},{24,28},{1,5},{5,9},{9,... | collective-permute-start | bytes 491528 | tf_op jit(solution)/shard_map/ppermute | solution.py:18
  102.8 1.8 %copy-start.1 = (bf16[2,320,2240]{2,1,0:T(8,128)(2,1)S(1)}, bf16[2,320,2240]{2,1,0:T(8,128)(2,1)}, u32[]{:S(2)}) copy-start(bf16[2,320,2240]{2,1,0:T(8,128)(2,1)} %copy-done) | copy-start | bytes 8601604
  104.3 1.1 copy-start.6
  106.4 7.4 %collective-permute-start.9 = (bf16[1,2,320,128]{3,2,1,0:T(8,128)(2,1)S(1)}, bf16[1,2,320,128]{3,2,1,0:T(8,128)(2,1)S(1)}, u32[]{:S(2)}, u32[]{:S(2)}) collective-permute-start(bf16[1,2,320,128]{3,2,1,0:T(8,128)(2,1)S(1)} %get-tuple-element.19), channel_id=1, source_target_pairs={{4,0},{8,4},{12,8},{16,12},{20,16},{24,20},{28,24},{5,1},{9,5},{13... | collective-permute-start | bytes 491528 | tf_op jit(solution)/shard_map/ppermute | solution.py:21
  109.6 5.4 %collective-permute-start.8 = (bf16[1,2,320,128]{3,2,1,0:T(8,128)(2,1)S(1)}, bf16[1,2,320,128]{3,2,1,0:T(8,128)(2,1)S(1)}, u32[]{:S(2)}, u32[]{:S(2)}) collective-permute-start(bf16[1,2,320,128]{3,2,1,0:T(8,128)(2,1)S(1)} %get-tuple-element.19), channel_id=1, source_target_pairs={{0,4},{4,8},{8,12},{12,16},{16,20},{20,24},{24,28},{1,5},{5,9},{9,... | collective-permute-start | bytes 491528 | tf_op jit(solution)/shard_map/ppermute | solution.py:18
  116.4 1.8 %copy-start.2 = (bf16[2,320,2240]{2,1,0:T(8,128)(2,1)S(1)}, bf16[2,320,2240]{2,1,0:T(8,128)(2,1)}, u32[]{:S(2)}) copy-start(bf16[2,320,2240]{2,1,0:T(8,128)(2,1)} %copy-done) | copy-start | bytes 8601604
  119.2 7.4 %collective-permute-start.11 = (bf16[1,2,320,128]{3,2,1,0:T(8,128)(2,1)S(1)}, bf16[1,2,320,128]{3,2,1,0:T(8,128)(2,1)S(1)}, u32[]{:S(2)}, u32[]{:S(2)}) collective-permute-start(bf16[1,2,320,128]{3,2,1,0:T(8,128)(2,1)S(1)} %get-tuple-element.17), channel_id=1, source_target_pairs={{4,0},{8,4},{12,8},{16,12},{20,16},{24,20},{28,24},{5,1},{9,5},{13... | collective-permute-start | bytes 491528 | tf_op jit(solution)/shard_map/ppermute | solution.py:21
  122.4 5.4 %collective-permute-start.10 = (bf16[1,2,320,128]{3,2,1,0:T(8,128)(2,1)S(1)}, bf16[1,2,320,128]{3,2,1,0:T(8,128)(2,1)S(1)}, u32[]{:S(2)}, u32[]{:S(2)}) collective-permute-start(bf16[1,2,320,128]{3,2,1,0:T(8,128)(2,1)S(1)} %get-tuple-element.17), channel_id=1, source_target_pairs={{0,4},{4,8},{8,12},{12,16},{16,20},{20,24},{24,28},{1,5},{5,9},{9,... | collective-permute-start | bytes 491528 | tf_op jit(solution)/shard_map/ppermute | solution.py:18
  129.2 1.8 %copy-start.3 = (bf16[2,320,2240]{2,1,0:T(8,128)(2,1)S(1)}, bf16[2,320,2240]{2,1,0:T(8,128)(2,1)}, u32[]{:S(2)}) copy-start(bf16[2,320,2240]{2,1,0:T(8,128)(2,1)} %copy-done) | copy-start | bytes 8601604
where the time goes:
time: 135 us; the launch traced here: 133 us
  waiting for transfers between devices  56.4 us (42%)
  starting transfers between devices  37.8 us (28%)
  local copies, waits for them, and re-layouts  16.8 us (12%)
  other arithmetic  13.3 us (10%)
  matrix products  6.75 us (5%)
  between operations  1.75 us (1%)
    ppermute x4, waiting for transfers between devices, from_behind(): lax.ppermute(value, axis, [(source, source + steps) for source in range(l...  47.7 us
    ppermute x4, starting transfers between devices, with_halo(): lax.ppermute(lax.slice_in_dim(block, 0, width, axis=dim), axis, backward)  13.8 us
    ppermute x4, starting transfers between devices, with_halo(): lax.ppermute(lax.slice_in_dim(block, block.shape[dim] - width, None, axis...  12.7 us
    ppermute x4, starting transfers between devices, from_behind(): lax.ppermute(value, axis, [(source, source + steps) for source in range(l...  11.3 us
    dot_general x4, matrix products, coupled(): jnp.einsum('nde,ner->ndr', row_blocks, stacked, preferred_element_type=jn...  6.75 us
    select_n x4, other arithmetic, turned_faces(): jnp.where((face_codes == quarter)[:, :, None, None, None, None, None], jn...  5.62 us
    concatenate x1, other arithmetic, shards(): jnp.concatenate([local_blocks, from_lower[0][None], from_upper[0][None]],...  5.01 us
    ppermute x4, waiting for transfers between devices, with_halo(): lax.ppermute(lax.slice_in_dim(block, block.shape[dim] - width, None, axis...  4.43 us
  transfers between devices with their start and end apart: 12, of which 10 were waited for; matrix products, arithmetic and copies ran while one was open for 6% of the time, Pallas kernels for 0%

commit v1 on v0

v1 whole, which is shorter than its diff:
```python
import functools
import jax
import jax.numpy as jnp
from jax import lax
from jax.experimental import pallas as pl
from jax.experimental.pallas import tpu as pltpu
from jax.sharding import PartitionSpec as P

NODES = 4
ITERS = 4
RELAXATION = 0.7
CHUNK = 32
TILE = 256
MESH = pl.DeviceIdType.MESH


def spans(width):
    return [(start, min(TILE, width - start)) for start in range(0, width, TILE)]


def turn_matrix(start, width, dof, codes):
    row = lax.broadcasted_iota(jnp.int32, (width, width), 0)
    col = lax.broadcasted_iota(jnp.int32, (width, width), 1)
    plane = NODES * NODES
    a = (row // plane) % NODES
    b = (row // NODES) % NODES
    rest = row - a * plane - b * NODES
    first, last = start // dof, (start + width - 1) // dof
    code = jnp.full((width, width), codes[first], jnp.int32)
    for segment in range(first + 1, last + 1):
        code = jnp.where(row < segment * dof - start, code, codes[segment])
    top = NODES - 1
    turned_a = jnp.where(code == 0, a, jnp.where(code == 1, b, jnp.where(code == 2, top - a, top - b)))
    turned_b = jnp.where(code == 0, b, jnp.where(code == 1, top - a, jnp.where(code == 2, top - b, a)))
    source = rest + turned_a * plane + turned_b * NODES
    return jnp.where(source == col, 1.0, 0.0).astype(jnp.bfloat16)


def kernel(layers, columns, blocks, rhs, departure, arrival, neighbors, orientation, out,
           local, local_rhs, leaving, leaving_rhs, near, near_rhs, far, far_rhs,
           kept, turns, stacked, current, kept_rhs, *rest):
    windows, sems = rest[:ITERS], rest[ITERS:]
    (load_sem, load_rhs_sem, near_send, near_recv, far_send, far_recv, rhs_send, rhs_recv,
     first_send, first_recv, halo_send, halo_recv) = sems
    slots, dof, width = local.shape
    rows = kept.shape[0]
    faces = width // dof - 1
    count = dof // CHUNK
    column, layer = lax.axis_index("gy"), lax.axis_index("gx")
    odd = lax.rem(column, 2)
    partner = column + 1 - 2 * odd
    onward = column + 2 - 4 * odd
    behind = column - 2 + 4 * odd
    has_onward = (onward >= 0) & (onward < columns)
    has_far = (behind >= 0) & (behind < columns)
    has_lower, has_upper = layer > 0, layer < layers - 1

    def part(index):
        return pl.ds(pl.multiple_of(index * CHUNK, CHUNK), CHUNK)

    def load(index):
        return pltpu.make_async_copy(blocks.at[:, part(index)], local.at[:, part(index)], load_sem.at[index])

    def send(source, target, send_sem, recv_sem, device):
        return pltpu.make_async_remote_copy(
            src_ref=source, dst_ref=target, send_sem=send_sem, recv_sem=recv_sem,
            device_id=device, device_id_type=MESH)

    def to_partner(index):
        return send(leaving.at[part(index)], near.at[part(index)], near_send.at[index], near_recv.at[index], {"gy": partner})

    def relay(index):
        return send(near.at[part(index)], far.at[part(index)], far_send.at[index], far_recv.at[index], {"gy": onward})

    rhs_to_partner = send(leaving_rhs, near_rhs, rhs_send.at[0], rhs_recv.at[0], {"gy": partner})
    rhs_relay = send(near_rhs, far_rhs, rhs_send.at[1], rhs_recv.at[1], {"gy": onward})

    def to_lower(source, target, send_sem, recv_sem):
        return send(source, target, send_sem, recv_sem, {"gx": layer - 1})

    def to_upper(source, target, send_sem, recv_sem):
        return send(source, target, send_sem, recv_sem, {"gx": layer + 1})

    def halo_down(sweep, row):
        window = windows[sweep]
        return to_lower(window.at[rows + row], window.at[2 * rows + row],
                        halo_send.at[sweep, 0, row], halo_recv.at[sweep, 0, row])

    def halo_up(sweep, row):
        window = windows[sweep]
        return to_upper(window.at[rows + row], window.at[row],
                        halo_send.at[sweep, 1, row], halo_recv.at[sweep, 1, row])

    def first_down(index):
        window = windows[1]
        return to_lower(window.at[pl.ds(rows, rows), part(index)], window.at[pl.ds(2 * rows, rows), part(index)],
                        first_send.at[0, index], first_recv.at[0, index])

    def first_up(index):
        window = windows[1]
        return to_upper(window.at[pl.ds(rows, rows), part(index)], window.at[pl.ds(0, rows), part(index)],
                        first_send.at[1, index], first_recv.at[1, index])

    load_rhs = pltpu.make_async_copy(rhs, local_rhs, load_rhs_sem)
    load_rhs.start()

    @pl.loop(0, count)
    def _(index):
        load(index).start()

    barrier = pltpu.get_barrier_semaphore()
    pl.semaphore_signal(barrier, inc=1, device_id={"gy": partner}, device_id_type=MESH)
    others = ((has_onward, {"gy": onward}), (has_far, {"gy": behind}),
              (has_lower, {"gx": layer - 1}), (has_upper, {"gx": layer + 1}))
    expected = 1
    for present, device in others:
        expected = expected + jnp.where(present, 1, 0)

        @pl.when(present)
        def _():
            pl.semaphore_signal(barrier, inc=1, device_id=device, device_id_type=MESH)
    pl.semaphore_wait(barrier, expected)

    slot = jnp.maximum(jnp.maximum(departure[0, 0, 0], departure[0, 0, 1]), 0)

    def pick(index, choices):
        value = choices[-1]
        for number in range(len(choices) - 2, -1, -1):
            value = lax.select(index == number, choices[number], value)
        return value

    load_rhs.wait()
    leaving_rhs[...] = pick(slot, [local_rhs[s] for s in range(slots)])
    rhs_to_partner.start()

    @pl.loop(0, count)
    def _(index):
        load(index).wait()
        leaving[part(index)] = pick(slot, [local[s, part(index)] for s in range(slots)])
        to_partner(index).start()

    for edge, missing in ((0, layer == 0), (2 * rows, layer == layers - 1)):
        @pl.when(missing)
        def _():
            for window in windows:
                window[pl.ds(edge, rows)] = jnp.zeros((rows,) + window.shape[1:], window.dtype)

    rhs_to_partner.wait_recv()

    @pl.when(has_onward)
    def _():
        rhs_relay.start()

    @pl.loop(0, rows)
    def _(row):
        codes = [0] + [orientation[0, 0, row, face] for face in range(faces)]
        for number, (start, size) in enumerate(spans(width)):
            turns[row, number, :size, :size] = turn_matrix(start, size, dof, codes)

    @pl.when(has_far)
    def _():
        rhs_relay.wait_recv()

    def pool_index(row):
        source = arrival[0, 0, row]
        return jnp.where(source < slots, source, jnp.where(source == slots + 1 - odd, slots, slots + 1))

    for row in range(rows):
        value = pick(pool_index(row), [local_rhs[s] for s in range(slots)] + [near_rhs[...], far_rhs[...]])
        value = value.astype(jnp.float32)
        kept_rhs[row] = value
        value = RELAXATION * value
        current[row] = value
        windows[0][rows + row] = value.astype(jnp.bfloat16)

    @pl.when(has_lower)
    def _():
        for row in range(rows):
            halo_down(0, row).start()

    @pl.when(has_upper)
    def _():
        for row in range(rows):
            halo_up(0, row).start()

    def stack(sweep):
        window = windows[sweep]
        for row in range(rows):
            stacked[row, :dof] = window[rows + row]
            for face in range(faces):
                stacked[row, (face + 1) * dof:(face + 2) * dof] = window[neighbors[0, 0, row, face]]

    def halo_wait(sweep):
        @pl.when(has_lower)
        def _():
            for row in range(rows):
                halo_up(sweep, row).wait_recv()

        @pl.when(has_upper)
        def _():
            for row in range(rows):
                halo_down(sweep, row).wait_recv()

    def take(index):
        to_partner(index).wait_recv()

        @pl.when(has_onward)
        def _():
            relay(index).start()

    take(0)
    halo_wait(0)
    stack(0)

    def process(index):
        @pl.when(has_far)
        def _():
            relay(index).wait_recv()

        here = part(index)
        for row in range(rows):
            source = pool_index(row)
            for number, (start, size) in enumerate(spans(width)):
                lanes = slice(start, start + size)
                value = pick(source, [local[s, here, lanes] for s in range(slots)] + [near[here, lanes], far[here, lanes]])
                kept[row, here, lanes] = jnp.dot(
                    value, turns[row, number, :size, :size], preferred_element_type=jnp.float32).astype(jnp.bfloat16)
            applied = jnp.dot(kept[row, here], stacked[row], preferred_element_type=jnp.float32)
            value = current[row, here] + RELAXATION * (kept_rhs[row, here] - applied)
            current[row, here] = value
            windows[1][rows + row, here] = value.astype(jnp.bfloat16)

        @pl.when(has_lower)
        def _():
            first_down(index).start()

        @pl.when(has_upper)
        def _():
            first_up(index).start()

    @pl.loop(1, count)
    def _(index):
        take(index)
        process(index - 1)

    process(count - 1)

    @pl.loop(0, count)
    def _(index):
        @pl.when(has_lower)
        def _():
            first_up(index).wait_recv()

        @pl.when(has_upper)
        def _():
            first_down(index).wait_recv()

    for sweep in range(1, ITERS):
        if sweep > 1:
            halo_wait(sweep)
        stack(sweep)
        for row in range(rows):
            applied = jnp.dot(kept[row], stacked[row], preferred_element_type=jnp.float32)
            value = current[row] + RELAXATION * (kept_rhs[row] - applied)
            if sweep == ITERS - 1:
                out[row] = value
                continue
            current[row] = value
            windows[sweep + 1][rows + row] = value.astype(jnp.bfloat16)

            @pl.when(has_lower)
            def _():
                halo_down(sweep + 1, row).start()

            @pl.when(has_upper)
            def _():
                halo_up(sweep + 1, row).start()

    rhs_to_partner.wait_send()

    @pl.when(has_onward)
    def _():
        rhs_relay.wait_send()

    @pl.loop(0, count)
    def _(index):
        to_partner(index).wait_send()

        @pl.when(has_onward)
        def _():
            relay(index).wait_send()

        @pl.when(has_lower)
        def _():
            first_down(index).wait_send()

        @pl.when(has_upper)
        def _():
            first_up(index).wait_send()

    for sweep in range(ITERS):
        if sweep == 1:
            continue

        @pl.when(has_lower)
        def _():
            for row in range(rows):
                halo_down(sweep, row).wait_send()

        @pl.when(has_upper)
        def _():
            for row in range(rows):
                halo_up(sweep, row).wait_send()


def solution(mesh):
    layers, columns = mesh.shape["gx"], mesh.shape["gy"]
    assert columns % 2 == 0

    def step(blocks, right_side, departure, arrival, neighbors, orientation):
        slots, dof, width = blocks.shape[2:]
        many = right_side.shape[-1]
        rows = arrival.shape[-1]
        count = dof // CHUNK
        bf16, f32, dma = jnp.bfloat16, jnp.float32, pltpu.SemaphoreType.DMA
        scratch = [
            pltpu.VMEM((slots, dof, width), bf16),
            pltpu.VMEM((slots, dof, many), bf16),
            pltpu.VMEM((dof, width), bf16),
            pltpu.VMEM((dof, many), bf16),
            pltpu.VMEM((dof, width), bf16),
            pltpu.VMEM((dof, many), bf16),
            pltpu.VMEM((dof, width), bf16),
            pltpu.VMEM((dof, many), bf16),
            pltpu.VMEM((rows, dof, width), bf16),
            pltpu.VMEM((rows, len(spans(width)), TILE, TILE), bf16),
            pltpu.VMEM((rows, width, many), bf16),
            pltpu.VMEM((rows, dof, many), f32),
            pltpu.VMEM((rows, dof, many), f32),
        ]
        scratch += [pltpu.VMEM((3 * rows, dof, many), bf16) for _ in range(ITERS)]
        scratch += [
            dma((count,)), dma(()), dma((count,)), dma((count,)), dma((count,)), dma((count,)), dma((2,)), dma((2,)),
            dma((2, count)), dma((2, count)), dma((ITERS, 2, rows)), dma((ITERS, 2, rows)),
        ]
        smem = pl.BlockSpec(memory_space=pltpu.SMEM)
        out = pl.pallas_call(
            functools.partial(kernel, layers, columns),
            out_shape=jax.ShapeDtypeStruct((rows, dof, many), f32),
            in_specs=[pl.BlockSpec(memory_space=pl.ANY)] * 2 + [smem] * 4,
            out_specs=pl.BlockSpec(memory_space=pltpu.VMEM),
            scratch_shapes=scratch,
            compiler_params=pltpu.CompilerParams(collective_id=0, has_side_effects=True),
        )(blocks[0, 0], right_side[0, 0], departure, arrival, neighbors, orientation)
        return out[None, None]

    in_specs = (
        P("gx", "gy", None, None, None),
        P("gx", "gy", None, None, None),
        P("gx", "gy", None),
        P("gx", "gy", None),
        P("gx", "gy", None, None),
        P("gx", "gy", None, None),
    )
    return jax.shard_map(step, mesh=mesh, in_specs=in_specs,
                         out_specs=P("gx", "gy", None, None, None), check_vma=False)
```

time: 135 us -> 61.8 us (0.46); the launches traced: 133 us -> 61.6 us
  Pallas kernels: 0 us -> 59.9 us
  waiting for transfers between devices: 56.4 us -> 0 us
  starting transfers between devices: 37.8 us -> 0 us
  local copies, waits for them, and re-layouts: 16.8 us -> 1.72 us
  other arithmetic: 13.3 us -> 0 us
  matrix products: 6.75 us -> 0 us
  between operations: 1.75 us -> 0.01 us
    pallas_call x0 -> x1, Pallas kernels: none -> 59.9 us  [step(): pl.pallas_call(functools.partial(kernel, layers, columns), out_shape=jax....]
    ppermute x12 -> x0, waiting for transfers between devices: 56.4 us -> none  [the longest x4 47.7 us: from_behind(): lax.ppermute(value, axis, [(source, source + steps) for source in range(l...]
    ppermute x12 -> x0, starting transfers between devices: 37.8 us -> none  [the longest x4 13.8 us: with_halo(): lax.ppermute(lax.slice_in_dim(block, 0, width, axis=dim), axis, backward)]
    gather x6 -> x0, local copies, waits for them, and re-layouts: 7.35 us -> none  [the longest x1 3.83 us: shards(): kept_blocks = jnp.take(block_pool, sources, axis=0)]
    dot_general x4 -> x0, matrix products: 6.75 us -> none  [coupled(): jnp.einsum('nde,ner->ndr', row_blocks, stacked, preferred_element_type=jn...]
    concatenate x10 -> x0, other arithmetic: 6.68 us -> none  [the longest x1 5.01 us: shards(): jnp.concatenate([local_blocks, from_lower[0][None], from_upper[0][None]],...]
    select_n x10 -> x0, other arithmetic: 6.25 us -> none  [the longest x4 5.62 us: turned_faces(): jnp.where((face_codes == quarter)[:, :, None, None, None, None, None], jn...]
    squeeze x2 -> x0, local copies, waits for them, and re-layouts: 4.63 us -> none  [the longest x1 3.66 us: shards(): local_blocks[upper_slot]]
  transfers between devices with their start and end apart: 12 -> 0, of which waited for: 10 -> 0; matrix products, arithmetic and copies ran while one was open for 6% -> 0% of each run, Pallas kernels for 0% -> 0%
where the time goes in v1:
time: 61.8 us; the launch traced here: 61.6 us
  Pallas kernels  59.9 us (97%)
  local copies, waits for them, and re-layouts  1.72 us (3%)
    pallas_call x1, Pallas kernels, step(): pl.pallas_call(functools.partial(kernel, layers, columns), out_shape=jax....  59.9 us
    unnamed x1, local copies, waits for them, and re-layouts  1.72 us

profile of v1, /device:TPU:11, one launch (start us, length us, event | category | flops | bytes accessed | tf_op | source)
XLA Modules:
  0.0 61.6 jit_solution(2487384928912812281)
XLA Ops:
  0.0 59.9 %shard_map.64 = f32[2,320,128]{2,1,0:T(8,128)} custom-call(bf16[3,320,2240]{2,1,0:T(8,128)(2,1)} %bitcast.3, bf16[3,320,128]{2,1,0:T(8,128)(2,1)} %bitcast.5, s32[1,1,2]{2,1,0:T(1,128)} %departure.1, s32[1,1,2]{2,1,0:T(1,128)} %arrival.1, s32[1,1,2,6]{3,2,1,0:T(2,128)} %neighbors.1, s32[1,1,2,6]{3,2,1,0:T(2,128)} %orientation.1), custom_call_target="tpu_custom_call" | custom-call | tf_op jit(solution)/shard_map/pallas_call | solution.py:347
  59.9 1.7 %copy.8 = f32[1,1,2,320,128]{4,3,2,1,0:T(8,128)} copy(f32[1,1,2,320,128]{4,3,2,1,0:T(8,128)} %bitcast.4) | data formatting | bytes 655360

commit v2 on v1

--- a/solution.py
+++ b/solution.py
@@ -9,13 +9,20 @@
 NODES = 4
 ITERS = 4
 RELAXATION = 0.7
-CHUNK = 32
+CHUNK = 16
+GROUP = 2
 TILE = 256
 MESH = pl.DeviceIdType.MESH
 
 
 def spans(width):
     return [(start, min(TILE, width - start)) for start in range(0, width, TILE)]
+
+
+def halves(dof):
+    block = NODES**3
+    first = -(-(dof // block) // 2) * block
+    return [(0, first), (first, dof - first)]
 
 
 def turn_matrix(start, width, dof, codes):
@@ -38,14 +45,18 @@
 
 def kernel(layers, columns, blocks, rhs, departure, arrival, neighbors, orientation, out,
            local, local_rhs, leaving, leaving_rhs, near, near_rhs, far, far_rhs,
-           kept, turns, stacked, current, kept_rhs, *rest):
-    windows, sems = rest[:ITERS], rest[ITERS:]
+           turns, current, kept_rhs, partial, *rest):
+    pieces = halves(local.shape[1])
+    kept, stacked = rest[:2], rest[2:4]
+    windows, sems = [rest[4 + 2 * sweep:6 + 2 * sweep] for sweep in range(ITERS)], rest[4 + 2 * ITERS:]
     (load_sem, load_rhs_sem, near_send, near_recv, far_send, far_recv, rhs_send, rhs_recv,
      first_send, first_recv, halo_send, halo_recv) = sems
     slots, dof, width = local.shape
-    rows = kept.shape[0]
+    rows = current.shape[0]
     faces = width // dof - 1
     count = dof // CHUNK
+    groups = count // GROUP
+    tall = CHUNK * GROUP
     column, layer = lax.axis_index("gy"), lax.axis_index("gx")
     odd = lax.rem(column, 2)
     partner = column + 1 - 2 * odd
@@ -81,25 +92,35 @@
     def to_upper(source, target, send_sem, recv_sem):
         return send(source, target, send_sem, recv_sem, {"gx": layer + 1})
 
-    def halo_down(sweep, row):
-        window = windows[sweep]
-        return to_lower(window.at[rows + row], window.at[2 * rows + row],
-                        halo_send.at[sweep, 0, row], halo_recv.at[sweep, 0, row])
-
-    def halo_up(sweep, row):
-        window = windows[sweep]
-        return to_upper(window.at[rows + row], window.at[row],
-                        halo_send.at[sweep, 1, row], halo_recv.at[sweep, 1, row])
-
-    def first_down(index):
-        window = windows[1]
-        return to_lower(window.at[pl.ds(rows, rows), part(index)], window.at[pl.ds(2 * rows, rows), part(index)],
-                        first_send.at[0, index], first_recv.at[0, index])
-
-    def first_up(index):
-        window = windows[1]
-        return to_upper(window.at[pl.ds(rows, rows), part(index)], window.at[pl.ds(0, rows), part(index)],
-                        first_send.at[1, index], first_recv.at[1, index])
+    own, low, high = pl.ds(rows, rows), pl.ds(0, rows), pl.ds(2 * rows, rows)
+
+    def halo_down(sweep, piece):
+        window = windows[sweep][piece]
+        return to_lower(window.at[own], window.at[high], halo_send.at[sweep, 0, piece], halo_recv.at[sweep, 0, piece])
+
+    def halo_up(sweep, piece):
+        window = windows[sweep][piece]
+        return to_upper(window.at[own], window.at[low], halo_send.at[sweep, 1, piece], halo_recv.at[sweep, 1, piece])
+
+    def inside(piece, group):
+        return pl.ds(pl.multiple_of(group * tall - pieces[piece][0], tall), tall)
+
+    def first_down(piece, group):
+        window, here = windows[1][piece], inside(piece, group)
+        return to_lower(window.at[own, here], window.at[high, here], first_send.at[0, group], first_recv.at[0, group])
+
+    def first_up(piece, group):
+        window, here = windows[1][piece], inside(piece, group)
+        return to_upper(window.at[own, here], window.at[low, here], first_send.at[1, group], first_recv.at[1, group])
+
+    def both(down, up):
+        @pl.when(has_lower)
+        def _():
+            down()
+
+        @pl.when(has_upper)
+        def _():
+            up()
 
     load_rhs = pltpu.make_async_copy(rhs, local_rhs, load_rhs_sem)
     load_rhs.start()
@@ -142,8 +163,9 @@
     for edge, missing in ((0, layer == 0), (2 * rows, layer == layers - 1)):
         @pl.when(missing)
         def _():
-            for window in windows:
-                window[pl.ds(edge, rows)] = jnp.zeros((rows,) + window.shape[1:], window.dtype)
+            for pair in windows:
+                for window in pair:
+                    window[pl.ds(edge, rows)] = jnp.zeros((rows,) + window.shape[1:], window.dtype)
 
     rhs_to_partner.wait_recv()
 
@@ -171,35 +193,25 @@
         kept_rhs[row] = value
         value = RELAXATION * value
         current[row] = value
-        windows[0][rows + row] = value.astype(jnp.bfloat16)
-
-    @pl.when(has_lower)
-    def _():
+        rounded = value.astype(jnp.bfloat16)
+        for piece, (start, size) in enumerate(pieces):
+            windows[0][piece][rows + row] = rounded[start:start + size]
+
+    def halo_start(sweep, piece):
+        both(lambda: halo_down(sweep, piece).start(), lambda: halo_up(sweep, piece).start())
+
+    def halo_wait(sweep, piece):
+        both(lambda: halo_up(sweep, piece).wait_recv(), lambda: halo_down(sweep, piece).wait_recv())
+
+    def stack(sweep, piece):
+        window, size = windows[sweep][piece], pieces[piece][1]
         for row in range(rows):
-            halo_down(0, row).start()
-
-    @pl.when(has_upper)
-    def _():
-        for row in range(rows):
-            halo_up(0, row).start()
-
-    def stack(sweep):
-        window = windows[sweep]
-        for row in range(rows):
-            stacked[row, :dof] = window[rows + row]
+            stacked[piece][row, :size] = window[rows + row]
             for face in range(faces):
-                stacked[row, (face + 1) * dof:(face + 2) * dof] = window[neighbors[0, 0, row, face]]
-
-    def halo_wait(sweep):
-        @pl.when(has_lower)
-        def _():
-            for row in range(rows):
-                halo_up(sweep, row).wait_recv()
-
-        @pl.when(has_upper)
-        def _():
-            for row in range(rows):
-                halo_down(sweep, row).wait_recv()
+                stacked[piece][row, (face + 1) * size:(face + 2) * size] = window[neighbors[0, 0, row, face]]
+
+    for piece in range(2):
+        halo_start(0, piece)
 
     def take(index):
         to_partner(index).wait_recv()
@@ -208,73 +220,75 @@
         def _():
             relay(index).start()
 
-    take(0)
-    halo_wait(0)
-    stack(0)
-
-    def process(index):
+    def take_group(group):
+        for member in range(GROUP):
+            take(group * GROUP + member)
+
+    take_group(0)
+    for piece in range(2):
+        halo_wait(0, piece)
+        stack(0, piece)
+
+    def process(piece, group):
         @pl.when(has_far)
         def _():
-            relay(index).wait_recv()
-
-        here = part(index)
+            for member in range(GROUP):
+                relay(group * GROUP + member).wait_recv()
+
+        here = pl.ds(pl.multiple_of(group * tall, tall), tall)
         for row in range(rows):
             source = pool_index(row)
+            turned = []
             for number, (start, size) in enumerate(spans(width)):
                 lanes = slice(start, start + size)
                 value = pick(source, [local[s, here, lanes] for s in range(slots)] + [near[here, lanes], far[here, lanes]])
-                kept[row, here, lanes] = jnp.dot(
-                    value, turns[row, number, :size, :size], preferred_element_type=jnp.float32).astype(jnp.bfloat16)
-            applied = jnp.dot(kept[row, here], stacked[row], preferred_element_type=jnp.float32)
+                turned.append(jnp.dot(
+                    value, turns[row, number, :size, :size], preferred_element_type=jnp.float32).astype(jnp.bfloat16))
+            turned = jnp.concatenate(turned, axis=1)
+            applied = 0.0
+            for part_of, (start, size) in enumerate(pieces):
+                value = jnp.concatenate(
+                    [turned[:, face * dof + start:face * dof + start + size] for face in range(faces + 1)], axis=1)
+                kept[part_of][row, here] = value
+                applied = applied + jnp.dot(value, stacked[part_of][row], preferred_element_type=jnp.float32)
             value = current[row, here] + RELAXATION * (kept_rhs[row, here] - applied)
             current[row, here] = value
-            windows[1][rows + row, here] = value.astype(jnp.bfloat16)
-
-        @pl.when(has_lower)
-        def _():
-            first_down(index).start()
-
-        @pl.when(has_upper)
-        def _():
-            first_up(index).start()
-
-    @pl.loop(1, count)
-    def _(index):
-        take(index)
-        process(index - 1)
-
-    process(count - 1)
-
-    @pl.loop(0, count)
-    def _(index):
-        @pl.when(has_lower)
-        def _():
-            first_up(index).wait_recv()
-
-        @pl.when(has_upper)
-        def _():
-            first_down(index).wait_recv()
+            windows[1][piece][rows + row, inside(piece, group)] = value.astype(jnp.bfloat16)
+        both(lambda: first_down(piece, group).start(), lambda: first_up(piece, group).start())
+
+    for piece, (start, size) in enumerate(pieces):
+        @pl.loop(start // tall, (start + size) // tall)
+        def _(group):
+            @pl.when(group + 1 < groups)
+            def _():
+                take_group(group + 1)
+            process(piece, group)
 
     for sweep in range(1, ITERS):
-        if sweep > 1:
-            halo_wait(sweep)
-        stack(sweep)
-        for row in range(rows):
-            applied = jnp.dot(kept[row], stacked[row], preferred_element_type=jnp.float32)
-            value = current[row] + RELAXATION * (kept_rhs[row] - applied)
-            if sweep == ITERS - 1:
-                out[row] = value
-                continue
-            current[row] = value
-            windows[sweep + 1][rows + row] = value.astype(jnp.bfloat16)
-
-            @pl.when(has_lower)
-            def _():
-                halo_down(sweep + 1, row).start()
-
-            @pl.when(has_upper)
-            def _():
-                halo_up(sweep + 1, row).start()
+        for piece, (start, size) in enumerate(pieces):
+            if sweep > 1:
+                halo_wait(sweep, piece)
+            else:
+                @pl.loop(start // tall, (start + size) // tall)
+                def _(group):
+                    both(lambda: first_up(piece, group).wait_recv(), lambda: first_down(piece, group).wait_recv())
+            stack(sweep, piece)
+            if piece == 0:
+                for row in range(rows):
+                    partial[row] = jnp.dot(kept[0][row], stacked[0][row], preferred_element_type=jnp.float32)
+        for piece, (start, size) in enumerate(pieces):
+            here = slice(start, start + size)
+            for row in range(rows):
+                applied = partial[row, here] + jnp.dot(
+                    kept[1][row, here], stacked[1][row], preferred_element_type=jnp.float32)
+                value = current[row, here] + RELAXATION * (kept_rhs[row, here] - applied)
+                if sweep == ITERS - 1:
+                    out[row, here] = value
+                    continue
+                current[row, here] = value
+                windows[sweep + 1][piece][rows + row] = value.astype(jnp.bfloat16)
+            if sweep < ITERS - 1:
+                halo_start(sweep + 1, piece)
 
     rhs_to_partner.wait_send()
 
@@ -290,27 +304,14 @@
         def _():
             relay(index).wait_send()
 
-        @pl.when(has_lower)
-        def _():
-            first_down(index).wait_send()
-
-        @pl.when(has_upper)
-        def _():
-            first_up(index).wait_send()
-
-    for sweep in range(ITERS):
-        if sweep == 1:
-            continue
-
-        @pl.when(has_lower)
-        def _():
-            for row in range(rows):
-                halo_down(sweep, row).wait_send()
-
-        @pl.when(has_upper)
-        def _():
-            for row in range(rows):
-                halo_up(sweep, row).wait_send()
+    for piece, (start, size) in enumerate(pieces):
+        @pl.loop(start // tall, (start + size) // tall)
+        def _(group):
+            both(lambda: first_down(piece, group).wait_send(), lambda: first_up(piece, group).wait_send())
+
+        for sweep in range(ITERS):
+            if sweep != 1:
+                both(lambda: halo_down(sweep, piece).wait_send(), lambda: halo_up(sweep, piece).wait_send())
 
 
 def solution(mesh):
@@ -332,16 +333,18 @@
             pltpu.VMEM((dof, many), bf16),
             pltpu.VMEM((dof, width), bf16),
             pltpu.VMEM((dof, many), bf16),
-            pltpu.VMEM((rows, dof, width), bf16),
             pltpu.VMEM((rows, len(spans(width)), TILE, TILE), bf16),
-            pltpu.VMEM((rows, width, many), bf16),
+            pltpu.VMEM((rows, dof, many), f32),
             pltpu.VMEM((rows, dof, many), f32),
             pltpu.VMEM((rows, dof, many), f32),
         ]
-        scratch += [pltpu.VMEM((3 * rows, dof, many), bf16) for _ in range(ITERS)]
+        sizes = [size for _, size in halves(dof)]
+        scratch += [pltpu.VMEM((rows, dof, width // dof * size), bf16) for size in sizes]
+        scratch += [pltpu.VMEM((rows, width // dof * size, many), bf16) for size in sizes]
+        scratch += [pltpu.VMEM((3 * rows, size, many), bf16) for _ in range(ITERS) for size in sizes]
         scratch += [
             dma((count,)), dma(()), dma((count,)), dma((count,)), dma((count,)), dma((count,)), dma((2,)), dma((2,)),
-            dma((2, count)), dma((2, count)), dma((ITERS, 2, rows)), dma((ITERS, 2, rows)),
+            dma((2, count // GROUP)), dma((2, count // GROUP)), dma((ITERS, 2, 2)), dma((ITERS, 2, 2)),
         ]
         smem = pl.BlockSpec(memory_space=pltpu.SMEM)
         out = pl.pallas_call(

time: 61.8 us -> 60.1 us (0.972)
  Pallas kernels: 59.9 us -> 58.2 us
    pallas_call x1, Pallas kernels: 59.9 us -> 58.2 us  [step(): pl.pallas_call(functools.partial(kernel, layers, columns), out_shape=jax....]
where the time goes in v2:
time: 60.1 us; the launch traced here: 59.9 us
  Pallas kernels  58.2 us (97%)
  local copies, waits for them, and re-layouts  1.72 us (3%)
    pallas_call x1, Pallas kernels, step(): pl.pallas_call(functools.partial(kernel, layers, columns), out_shape=jax....  58.2 us
    unnamed x1, local copies, waits for them, and re-layouts  1.72 us

profile of v2, /device:TPU:11, one launch (start us, length us, event | category | flops | bytes accessed | tf_op | source)
XLA Modules:
  0.0 59.9 jit_solution(9120568183752930023)
XLA Ops:
  0.0 58.2 %shard_map.64 = f32[2,320,128]{2,1,0:T(8,128)} custom-call(bf16[3,320,2240]{2,1,0:T(8,128)(2,1)} %bitcast.3, bf16[3,320,128]{2,1,0:T(8,128)(2,1)} %bitcast.5, s32[1,1,2]{2,1,0:T(1,128)} %departure.1, s32[1,1,2]{2,1,0:T(1,128)} %arrival.1, s32[1,1,2,6]{3,2,1,0:T(2,128)} %neighbors.1, s32[1,1,2,6]{3,2,1,0:T(2,128)} %orientation.1), custom_call_target="tpu_custom_call" | custom-call | tf_op jit(solution)/shard_map/pallas_call | solution.py:350
  58.2 1.7 %copy.8 = f32[1,1,2,320,128]{4,3,2,1,0:T(8,128)} copy(f32[1,1,2,320,128]{4,3,2,1,0:T(8,128)} %bitcast.4) | data formatting | bytes 655360

commit v3 on v2

--- a/solution.py
+++ b/solution.py
@@ -21,7 +21,7 @@
 
 def halves(dof):
     block = NODES**3
-    first = -(-(dof // block) // 2) * block
+    first = dof // block // 2 * block
     return [(0, first), (first, dof - first)]
 
 
@@ -43,14 +43,15 @@
     return jnp.where(source == col, 1.0, 0.0).astype(jnp.bfloat16)
 
 
-def kernel(layers, columns, blocks, rhs, departure, arrival, neighbors, orientation, out,
+def kernel(layers, columns, blocks, rhs, departure_in, arrival_in, neighbors_in, orientation_in, out,
+           departure, arrival, neighbors, orientation,
            local, local_rhs, leaving, leaving_rhs, near, near_rhs, far, far_rhs,
            turns, current, kept_rhs, partial, *rest):
     pieces = halves(local.shape[1])
     kept, stacked = rest[:2], rest[2:4]
     windows, sems = [rest[4 + 2 * sweep:6 + 2 * sweep] for sweep in range(ITERS)], rest[4 + 2 * ITERS:]
     (load_sem, load_rhs_sem, near_send, near_recv, far_send, far_recv, rhs_send, rhs_recv,
-     first_send, first_recv, halo_send, halo_recv) = sems
+     first_send, first_recv, halo_send, halo_recv, plan_sem) = sems
     slots, dof, width = local.shape
     rows = current.shape[0]
     faces = width // dof - 1
@@ -77,11 +78,16 @@
             src_ref=source, dst_ref=target, send_sem=send_sem, recv_sem=recv_sem,
             device_id=device, device_id_type=MESH)
 
-    def to_partner(index):
-        return send(leaving.at[part(index)], near.at[part(index)], near_send.at[index], near_recv.at[index], {"gy": partner})
-
-    def relay(index):
-        return send(near.at[part(index)], far.at[part(index)], far_send.at[index], far_recv.at[index], {"gy": onward})
+    middle = -(-width // TILE) * TILE // 2
+    sides = (slice(0, middle), slice(middle, width))
+
+    def to_partner(index, side):
+        here, lanes = part(index), sides[side]
+        return send(leaving.at[here, lanes], near.at[here, lanes], near_send.at[side, index], near_recv.at[side, index], {"gy": partner})
+
+    def relay(index, side):
+        here, lanes = part(index), sides[side]
+        return send(near.at[here, lanes], far.at[here, lanes], far_send.at[side, index], far_recv.at[side, index], {"gy": onward})
 
     rhs_to_partner = send(leaving_rhs, near_rhs, rhs_send.at[0], rhs_recv.at[0], {"gy": partner})
     rhs_relay = send(near_rhs, far_rhs, rhs_send.at[1], rhs_recv.at[1], {"gy": onward})
@@ -124,6 +130,10 @@
 
     load_rhs = pltpu.make_async_copy(rhs, local_rhs, load_rhs_sem)
     load_rhs.start()
+    plans = [pltpu.make_async_copy(source, target, plan_sem.at[number]) for number, (source, target) in enumerate((
+        (departure_in, departure), (arrival_in, arrival), (neighbors_in, neighbors), (orientation_in, orientation)))]
+    for plan in plans:
+        plan.start()
 
     @pl.loop(0, count)
     def _(index):
@@ -142,6 +152,8 @@
             pl.semaphore_signal(barrier, inc=1, device_id=device, device_id_type=MESH)
     pl.semaphore_wait(barrier, expected)
 
+    for plan in plans:
+        plan.wait()
     slot = jnp.maximum(jnp.maximum(departure[0, 0, 0], departure[0, 0, 1]), 0)
 
     def pick(index, choices):
@@ -158,7 +170,8 @@
     def _(index):
         load(index).wait()
         leaving[part(index)] = pick(slot, [local[s, part(index)] for s in range(slots)])
-        to_partner(index).start()
+        for side in range(2):
+            to_partner(index, side).start()
 
     for edge, missing in ((0, layer == 0), (2 * rows, layer == layers - 1)):
         @pl.when(missing)
@@ -214,11 +227,12 @@
         halo_start(0, piece)
 
     def take(index):
-        to_partner(index).wait_recv()
-
-        @pl.when(has_onward)
-        def _():
-            relay(index).start()
+        for side in range(2):
+            to_partner(index, side).wait_recv()
+
+            @pl.when(has_onward)
+            def _():
+                relay(index, side).start()
 
     def take_group(group):
         for member in range(GROUP):
@@ -233,7 +247,8 @@
         @pl.when(has_far)
         def _():
             for member in range(GROUP):
-                relay(group * GROUP + member).wait_recv()
+                for side in range(2):
+                    relay(group * GROUP + member, side).wait_recv()
 
         here = pl.ds(pl.multiple_of(group * tall, tall), tall)
         for row in range(rows):
@@ -298,11 +313,12 @@
 
     @pl.loop(0, count)
     def _(index):
-        to_partner(index).wait_send()
-
-        @pl.when(has_onward)
-        def _():
-            relay(index).wait_send()
+        for side in range(2):
+            to_partner(index, side).wait_send()
+
+            @pl.when(has_onward)
+            def _():
+                relay(index, side).wait_send()
 
     for piece, (start, size) in enumerate(pieces):
         @pl.loop(start // tall, (start + size) // tall)
@@ -324,7 +340,8 @@
         rows = arrival.shape[-1]
         count = dof // CHUNK
         bf16, f32, dma = jnp.bfloat16, jnp.float32, pltpu.SemaphoreType.DMA
-        scratch = [
+        scratch = [pltpu.SMEM(plan.shape, plan.dtype) for plan in (departure, arrival, neighbors, orientation)]
+        scratch += [
             pltpu.VMEM((slots, dof, width), bf16),
             pltpu.VMEM((slots, dof, many), bf16),
             pltpu.VMEM((dof, width), bf16),
@@ -343,14 +360,13 @@
         scratch += [pltpu.VMEM((rows, width // dof * size, many), bf16) for size in sizes]
         scratch += [pltpu.VMEM((3 * rows, size, many), bf16) for _ in range(ITERS) for size in sizes]
         scratch += [
-            dma((count,)), dma(()), dma((count,)), dma((count,)), dma((count,)), dma((count,)), dma((2,)), dma((2,)),
-            dma((2, count // GROUP)), dma((2, count // GROUP)), dma((ITERS, 2, 2)), dma((ITERS, 2, 2)),
+            dma((count,)), dma(()), dma((2, count)), dma((2, count)), dma((2, count)), dma((2, count)), dma((2,)), dma((2,)),
+            dma((2, count // GROUP)), dma((2, count // GROUP)), dma((ITERS, 2, 2)), dma((ITERS, 2, 2)), dma((4,)),
         ]
-        smem = pl.BlockSpec(memory_space=pltpu.SMEM)
         out = pl.pallas_call(
             functools.partial(kernel, layers, columns),
             out_shape=jax.ShapeDtypeStruct((rows, dof, many), f32),
-            in_specs=[pl.BlockSpec(memory_space=pl.ANY)] * 2 + [smem] * 4,
+            in_specs=[pl.BlockSpec(memory_space=pl.ANY)] * 6,
             out_specs=pl.BlockSpec(memory_space=pltpu.VMEM),
             scratch_shapes=scratch,
             compiler_params=pltpu.CompilerParams(collective_id=0, has_side_effects=True),

time: 60.1 us -> 59.5 us (0.990)
  no operation moved by 1% of the time
where the time goes in v3:
time: 59.5 us; the launch traced here: 59.4 us
  Pallas kernels  57.7 us (97%)
  local copies, waits for them, and re-layouts  1.72 us (3%)
    pallas_call x1, Pallas kernels, step(): pl.pallas_call(functools.partial(kernel, layers, columns), out_shape=jax....  57.7 us
    unnamed x1, local copies, waits for them, and re-layouts  1.72 us

profile of v3, /device:TPU:11, one launch (start us, length us, event | category | flops | bytes accessed | tf_op | source)
XLA Modules:
  0.0 59.4 jit_solution(8765767140330824180)
XLA Ops:
  0.0 57.7 %shard_map.64 = f32[2,320,128]{2,1,0:T(8,128)} custom-call(bf16[3,320,2240]{2,1,0:T(8,128)(2,1)} %bitcast.3, bf16[3,320,128]{2,1,0:T(8,128)(2,1)} %bitcast.5, s32[1,1,2]{2,1,0:T(1,128)} %departure_in.1, s32[1,1,2]{2,1,0:T(1,128)} %arrival_in.1, s32[1,1,2,6]{3,2,1,0:T(2,128)} %neighbors_in.1, s32[1,1,2,6]{3,2,1,0:T(2,128)} %orientation_in.1), custom_call_target="tpu_custom_call" | custom-call | tf_op jit(solution)/shard_map/pallas_call | solution.py:366
  57.7 1.7 %copy.8 = f32[1,1,2,320,128]{4,3,2,1,0:T(8,128)} copy(f32[1,1,2,320,128]{4,3,2,1,0:T(8,128)} %bitcast.4) | data formatting | bytes 655360
